TPU v7x, 1024 devices: a whole 4x8x16 slice. The times are simulated.
1024 devices in a mesh: pair: 128 (over z_lo, y, core), aux: 8 (over x, z_hi).
Axes of the slice: x: 4, y: 8, z: 16 (z_hi: 2, z_lo: 8; z = z_hi * 8 + z_lo), core: 2. Of those that a mesh axis runs over, the one named last changes fastest.
Arguments:
- occupied_index: int32 [128], P('pair'), may hold values from 0 to 3
- doubles_slab: bfloat16 [128, 2048, 2048], P('pair', 'aux'), may hold values from -0.015625 to 0.015625
- lambda_slab: bfloat16 [128, 2048, 2048], P('pair', 'aux'), may hold values from -0.015625 to 0.015625
- aux_factors: bfloat16 [128, 256, 2048], P('pair'), may hold values from -24 to 24
- dressed_factors: bfloat16 [128, 256, 2048], P('pair'), may hold values from -6 to 6
- virtual_coefs: bfloat16 [1024, 2048], P(None, 'aux'), may hold values from -0.125 to 0.125
- occupied_coefs: float32 [512, 4], replicated, may hold values from -3 to 3
Outputs:
- gamma_basis: bfloat16 [256, 512, 1024], P('pair', None, 'aux')
Inputs may be any that keep to these rules, and one draw needn't show every extreme that they name: `occupied_index`: entry p is the occupied index i that forms a pair with the occupied index j = p.
All inputs are finite; a program needn't handle non-finite values.
Results may differ from a plain program's by a relative error of at most 0.014.
Values may be sent and summed in bfloat16 or wider, within the bound.
A program may use at most 32 MiB of HBM per device.

v0:
```python
import jax
import jax.numpy as jnp
from jax import lax
from jax.sharding import PartitionSpec as P

I_WIN = 4


def side_by_side(arrays, axis, split_dim, concat_dim, along):
    columns = [a.reshape(*a.shape[:along], -1) for a in arrays]
    both = jnp.concatenate(columns, axis=along)
    out, at, outs = (
        lax.all_to_all(both, axis, split_axis=split_dim, concat_axis=concat_dim, tiled=True),
        0,
        [],
    )
    for a, column in zip(arrays, columns):
        share = out[..., at : at + column.shape[along]]
        outs.append(share.reshape(*share.shape[:along], *a.shape[along:]))
        at += column.shape[along]
    return tuple(outs)


def in_blocks(array, dim, count):
    dims = array.shape
    tiles = array.reshape(*dims[:dim], count, dims[dim] // count, *dims[dim + 1 :])
    return jnp.moveaxis(tiles, dim, 0)


def sum_at_owner(array, axis, dim):
    tiles = in_blocks(array, dim, lax.axis_size(axis))
    arrived = lax.all_to_all(tiles, axis, split_axis=0, concat_axis=0, tiled=True)
    return arrived.astype(jnp.float32).sum(axis=0)


def shards(
    occupied_index,
    doubles_slab,
    lambda_slab,
    aux_factors,
    dressed_factors,
    virtual_coefs,
    occupied_coefs,
):
    first_amps = doubles_slab[0]
    second_amps = lambda_slab[0]
    factor_one = aux_factors[0]
    factor_two = dressed_factors[0]
    contract = (((1,), (1,)), ((), ()))
    groups = lax.axis_size("pair")
    product = lax.dot_general(factor_one, first_amps, contract, preferred_element_type=jnp.float32)
    product = product + lax.dot_general(
        factor_two, second_amps, contract, preferred_element_type=jnp.float32
    )
    grouped = product.reshape(groups, product.shape[0] // groups, product.shape[1])
    index_column = jnp.broadcast_to(occupied_index[0].astype(jnp.float32), (groups, 1))
    received, sender_index = side_by_side((grouped, index_column), "pair", 0, 0, 1)
    levels = jnp.arange(I_WIN).astype(jnp.float32)
    onehot = (sender_index[:, 0][:, None] == levels[None, :]).astype(jnp.float32)
    summed = jnp.einsum("pi,pqa->qia", onehot, received, precision=lax.Precision.HIGHEST)
    gamma_mo = summed.astype(jnp.bfloat16)
    virtual_term = jnp.einsum(
        "qia,na->qin", gamma_mo, virtual_coefs, preferred_element_type=jnp.float32
    )
    half_back = sum_at_owner(virtual_term.astype(jnp.bfloat16), "aux", 2)
    gamma_basis = jnp.einsum(
        "mi,qin->qmn", occupied_coefs, half_back, precision=lax.Precision.HIGHEST
    )
    return gamma_basis.astype(jnp.bfloat16)


def solution(mesh):
    placed = (
        P("pair"),
        P("pair", "aux", None),
        P("pair", "aux", None),
        P("pair", None, None),
        P("pair", None, None),
        P(None, "aux"),
        P(),
    )
    return jax.shard_map(
        shards, mesh=mesh, in_specs=placed, out_specs=P("pair", None, "aux"), check_vma=False
    )
```

profile of v0, /device:TPU:1, one launch (start us, length us, event | category | flops | bytes accessed | tf_op | source)
XLA Modules:
  0.0 84.5 jit_solution(11782103457158145938)
XLA Ops:
  0.0 0.0 copy-start
  0.0 0.0 copy-start.2
  0.0 0.0 copy-start.1
  0.0 1.2 %copy-done = bf16[1,256,2048]{2,1,0:T(8,128)(2,1)S(1)} copy-done((bf16[1,256,2048]{2,1,0:T(8,128)(2,1)S(1)}, bf16[1,256,2048]{2,1,0:T(8,128)(2,1)}, u32[]{:S(2)}) %copy-start) | copy-done | bytes 1048600
  1.2 1.7 %fusion.5 = f32[256,256]{1,0:T(8,128)S(1)} fusion(bf16[1,256,2048]{2,1,0:T(8,128)(2,1)S(1)} %copy-done, bf16[1,256,2048]{2,1,0:T(8,128)(2,1)} %param.10), kind=kOutput, calls=%fused_computation.9 | convolution fusion | flops 268435456 | bytes 2359296 | tf_op jit(solution)/shard_map/dot_general | solution.py:51
  2.9 0.0 copy-done.2
  2.9 0.0 copy-done.1
  2.9 0.5 convolution_add_fusion
  3.4 0.1 reshape_reshape.3
  3.5 0.1 copy.17
  4.3 0.9 %copy.18 = f32[128,1,513]{2,1,0:T(1,128)} copy(f32[128,1,513]{0,2,1:T(8,128)S(1)} %pad_bitcast_fusion) | data formatting | bytes 525312 | tf_op jit(solution)/shard_map/all_to_all | solution.py:13
  5.2 23.8 %all-to-all-start = ((f32[128,1,513]{2,1,0:T(1,128)}), f32[128,1,513]{2,1,0:T(1,128)S(1)}, u32[]{:S(2)}, u32[]{:S(2)}) async-start(f32[128,1,513]{2,1,0:T(1,128)} %copy.18), calls=%async_computation | async-start | bytes 655360 | tf_op jit(solution)/shard_map/all_to_all | solution.py:13
  29.0 24.8 %all-to-all-done = f32[128,1,513]{2,1,0:T(1,128)S(1)} async-done(((f32[128,1,513]{2,1,0:T(1,128)}), f32[128,1,513]{2,1,0:T(1,128)S(1)}, u32[]{:S(2)}, u32[]{:S(2)}) %all-to-all-start) | async-done | bytes 262688 | tf_op jit(solution)/shard_map/all_to_all | solution.py:13
  53.8 0.2 copy.19
  54.0 0.0 copy-start.3
  54.0 0.2 fusion.2
  54.3 0.8 copy-done.3
  55.0 0.2 fusion.1
  55.3 27.0 %all_to_all.17 = bf16[8,2,4,128]{3,2,1,0:T(4,128)(2,1)S(1)} all-to-all(bf16[8,2,4,128]{3,2,1,0:T(4,128)(2,1)S(1)} %bitcast.46), channel_id=1, replica_groups=mesh['pair'=128,'aux'=8] {'aux'}, dimensions={0} | all-to-all | bytes 32768 | tf_op jit(solution)/shard_map/all_to_all | solution.py:32
  82.3 0.0 copy-start.4
  82.3 0.7 copy-done.4
  83.0 0.6 fusion
  83.6 0.8 copy.22
  (6 shorter events, 0.1 us)
Async XLA Ops:
  0.0 1.2 %copy-start = (bf16[1,256,2048]{2,1,0:T(8,128)(2,1)S(1)}, bf16[1,256,2048]{2,1,0:T(8,128)(2,1)}, u32[]{:S(2)}) copy-start(bf16[1,256,2048]{2,1,0:T(8,128)(2,1)} %param.8) | copy-start | bytes 3145732
  0.0 2.9 %copy-start.2 = (bf16[1,256,2048]{2,1,0:T(8,128)(2,1)S(1)}, bf16[1,256,2048]{2,1,0:T(8,128)(2,1)}, u32[]{:S(2)}) copy-start(bf16[1,256,2048]{2,1,0:T(8,128)(2,1)} %param.11) | copy-start | bytes 3145732
  0.0 2.9 %copy-start.1 = (bf16[1,256,2048]{2,1,0:T(8,128)(2,1)S(1)}, bf16[1,256,2048]{2,1,0:T(8,128)(2,1)}, u32[]{:S(2)}) copy-start(bf16[1,256,2048]{2,1,0:T(8,128)(2,1)} %param.9) | copy-start | bytes 3145732
  5.2 48.6 %all-to-all-start = ((f32[128,1,513]{2,1,0:T(1,128)}), f32[128,1,513]{2,1,0:T(1,128)S(1)}, u32[]{:S(2)}, u32[]{:S(2)}) async-start(f32[128,1,513]{2,1,0:T(1,128)} %copy.18), calls=%async_computation | async-start | bytes 655360 | tf_op jit(solution)/shard_map/all_to_all | solution.py:13
  54.0 1.0 %copy-start.3 = (bf16[1024,256]{1,0:T(8,128)(2,1)S(1)}, bf16[1024,256]{1,0:T(8,128)(2,1)}, u32[]{:S(2)}) copy-start(bf16[1024,256]{1,0:T(8,128)(2,1)} %param.12) | copy-start | bytes 1572868
  82.3 0.7 copy-start.4
where the time goes:
time: 84.8 us; the launch traced here: 84.5 us
  blocking collectives  27 us (32%)
  waiting for transfers between devices  24.8 us (29%)
  starting transfers between devices  23.8 us (28%)
  local copies, waits for them, and re-layouts  4.8 us (6%)
  matrix products  3.27 us (4%)
    all_to_all x1, blocking collectives, sum_at_owner(): lax.all_to_all(tiles, axis, split_axis=0, concat_axis=0, tiled=True)  27 us
    all_to_all x1, waiting for transfers between devices, side_by_side(): lax.all_to_all(both, axis, split_axis=split_dim, concat_axis=concat_dim,...  24.8 us
    all_to_all x1, starting transfers between devices, side_by_side(): lax.all_to_all(both, axis, split_axis=split_dim, concat_axis=concat_dim,...  23.8 us
    unnamed x10, local copies, waits for them, and re-layouts  2.67 us
  transfers between devices with their start and end apart: 1, of which 1 were waited for; matrix products, arithmetic and copies ran while one was open for 0% of the time, Pallas kernels for 0%

commit v1 on v0

v1 whole, which is shorter than its diff:
```python
import functools

import jax
import jax.numpy as jnp
from jax import lax
from jax.experimental import pallas as pl
from jax.experimental.pallas import tpu as pltpu
from jax.sharding import PartitionSpec as P

MESH = pl.DeviceIdType.MESH
F32, BF16 = jnp.float32, jnp.bfloat16
NT = (((1,), (1,)), ((), ()))
NX, NY, NZ, ZL = 4, 8, 16, 8
NR = 2 * NY


def device(x, y, z, core):
    pair = (lax.rem(z, ZL) * NY + y) * 2 + core
    aux = x * 2 + lax.div(z, ZL)
    return (pair, aux)


def kernel(
    idx_hbm, d_hbm, l_hbm, f_hbm, g_hbm, v_hbm, c_hbm, out_ref,
    idx_s, d_v, l_v, f_v, g_v, v_v, c_v,
    prod, idx_send, idx_recv, y_send, y_recv, sel, own_t, x_send, x_recv,
    total, z_send, z_recv, wide, left,
    load_sem, idx_sem, y_sem, x_sem, z_sem, ready_sem,
):
    pair, aux = lax.axis_index("pair"), lax.axis_index("aux")
    core = lax.rem(pair, 2)
    y = lax.rem(lax.div(pair, 2), NY)
    x = lax.div(aux, 2)
    z = lax.rem(aux, 2) * ZL + lax.div(pair, NR)
    barrier = pltpu.get_barrier_semaphore()

    def rel_y(dy, dc):
        return lax.rem(y + dy, NY), lax.rem(core + dc, 2)

    def dev_y(dy, dc):
        to_y, to_core = rel_y(dy, dc)
        return device(x, to_y, z, to_core)

    def dev_x(dx):
        return device(lax.rem(x + dx, NX), y, z, core)

    def dev_z(dz):
        return device(x, y, lax.rem(z + dz, NZ), core)

    def greet(to):
        pl.semaphore_signal(barrier, inc=1, device_id=to, device_id_type=MESH)

    @pl.loop(1, NR)
    def _(s):
        greet(dev_y(lax.div(s, 2), lax.rem(s, 2)))

    @pl.loop(1, NX)
    def _(s):
        greet(dev_x(s))

    @pl.loop(1, 5)
    def _(s):
        greet(dev_z(s))
        greet(dev_z(NZ - s))

    def load(src, dst, n):
        return pltpu.make_async_copy(src, dst, load_sem.at[n])

    half = d_v.shape[1] // 2
    loads = []
    for n, (a_hbm, a_v) in enumerate(((d_hbm, d_v), (f_hbm, f_v), (l_hbm, l_v), (g_hbm, g_v))):
        for k in range(2):
            cols = pl.ds(k * half, half)
            loads.append(load(a_hbm.at[0, :, cols], a_v.at[:, cols], n * 2 + k))
    for n in (0, 2, 1, 3, 4, 6, 5, 7):
        loads[n].start()
    load_v = load(v_hbm, v_v, 8)
    load_c = load(c_hbm, c_v, 9)
    load_i = load(idx_hbm, idx_s, 10)
    load_i.start()
    load_v.start()
    load_c.start()

    load_i.wait()
    idx_send[...] = jnp.full((1, 128), idx_s[0], jnp.int32)
    idx_recv[0] = jnp.full((1, 128), idx_s[0], jnp.int32)

    acc = None
    for n, (a_v, b_v) in enumerate(((f_v, d_v), (g_v, l_v))):
        for k in range(2):
            loads[n * 4 + k].wait()
            loads[n * 4 + 2 + k].wait()
            cols = slice(k * half, (k + 1) * half)
            part = lax.dot_general(a_v[:, cols], b_v[:, cols], NT, preferred_element_type=F32)
            acc = part if acc is None else acc + part
    prod[0] = acc[:, :128]
    prod[1] = acc[:, 128:]

    for r in range(NR):
        for j in range(2):
            even = prod[j, pl.ds(2 * r, 8, stride=32), :]
            odd = prod[j, pl.ds(2 * r + 1, 8, stride=32), :]
            both = jnp.concatenate([even, odd], axis=0).astype(BF16)
            y_send[r, :, j * 128 : (j + 1) * 128] = both
    y_recv[0] = y_send[y * 2 + core]

    pl.semaphore_wait(barrier, NR - 1 + NX - 1 + 8)

    for dz in (4, NZ - 4):
        pl.semaphore_signal(ready_sem, inc=1, device_id=dev_z(dz), device_id_type=MESH)

    def send_idx(dy, dc):
        pltpu.make_async_remote_copy(
            src_ref=idx_send, dst_ref=idx_recv.at[dy * 2 + dc],
            send_sem=idx_sem.at[0], recv_sem=idx_sem.at[1],
            device_id=dev_y(dy, dc), device_id_type=MESH,
        ).start()

    def send_y(dy, dc):
        to_y, to_core = rel_y(dy, dc)
        pltpu.make_async_remote_copy(
            src_ref=y_send.at[to_y * 2 + to_core], dst_ref=y_recv.at[dy * 2 + dc],
            send_sem=y_sem.at[0], recv_sem=y_sem.at[1],
            device_id=dev_y(dy, dc), device_id_type=MESH,
        ).start()

    def far_first(k):
        step = lax.div(k + 1, 2)
        return 4 + step - 2 * step * lax.rem(k, 2)

    for send in (send_idx, send_y):
        @pl.loop(0, NY - 1)
        def _(k):
            send(far_first(k), 0)
            send(far_first(k), 1)

        send(0, 1)

    load_c.wait()
    wide[...] = jnp.zeros_like(wide)
    c_hi = c_v[...].astype(BF16).astype(F32)
    c_lo = (c_v[...] - c_hi)
    for e in range(2):
        cols = slice(e * 512, (e + 1) * 512)
        for i in range(4):
            row = i * 2 + e
            wide[row : row + 1, cols] = c_hi[i : i + 1, :]
            wide[8 + row : 9 + row, cols] = c_hi[i : i + 1, :]
            wide[16 + row : 17 + row, cols] = c_lo[i : i + 1, :]
    left[...] = wide[...].T.astype(BF16)

    pltpu.make_async_copy(idx_recv.at[pl.ds(1, NR - 1)], idx_recv.at[pl.ds(1, NR - 1)], idx_sem.at[1]).wait()
    row = lax.broadcasted_iota(jnp.int32, (64, 256), 0)
    col = lax.broadcasted_iota(jnp.int32, (64, 256), 1)
    same = ((row >> 3) == (col & 7)) & ((row & 1) == ((col >> 3) & 1))
    lane = lax.broadcasted_iota(jnp.int32, (1, 128), 1) >> 4
    held = []
    for j in range(2):
        which = jnp.zeros((1, 128), jnp.int32)
        for s in range(8):
            which = which + idx_recv[j * 8 + s] * (lane == s).astype(jnp.int32)
        held.append(which)
    which = jnp.concatenate(held, axis=1)
    match = same.astype(F32) * (which == ((row >> 1) & 3)).astype(F32)
    sel[...] = match.astype(BF16)
    load_v.wait()

    pltpu.make_async_copy(y_recv.at[pl.ds(1, NR - 1)], y_recv.at[pl.ds(1, NR - 1)], y_sem.at[1]).wait()
    arrived = y_recv[...].reshape(256, 256)
    summed = jnp.dot(sel[...], arrived, preferred_element_type=F32).astype(BF16)

    def copy_x(dx):
        return pltpu.make_async_remote_copy(
            src_ref=x_send.at[dx - 1], dst_ref=x_recv.at[dx - 1],
            send_sem=x_sem.at[0, dx - 1], recv_sem=x_sem.at[1, dx - 1],
            device_id=dev_x(dx), device_id_type=MESH,
        )

    def turned(dx):
        rows = pl.ds(pl.multiple_of(lax.rem(x + dx, NX) * 256, 256), 256)
        return lax.dot_general(summed, v_v[rows, :], NT, preferred_element_type=F32)

    for dx in (2, 1, 3):
        x_send[dx - 1] = turned(dx).astype(BF16)
    for dx in (2, 1, 3):
        copy_x(dx).start()
    mine = turned(0)
    for dx in (1, 3, 2):
        copy_x(dx).wait_recv()
        mine = mine + x_recv[dx - 1].astype(F32)
    total[...] = mine.reshape(8, 8, 256)

    def z_block(dz):
        to_z = lax.rem(z + dz, NZ)
        cols = pl.ds(pl.multiple_of(lax.div(to_z, ZL) * 128, 128), 128)
        return total[lax.rem(to_z, ZL), :, cols]

    for dz in range(1, NZ):
        z_send[dz] = z_block(dz).astype(BF16)
    pl.semaphore_wait(ready_sem, 2)

    @pl.loop(0, NZ - 1)
    def _(k):
        step = lax.div(k + 1, 2)
        dz = 8 + step - 2 * step * lax.rem(k, 2)
        pltpu.make_async_remote_copy(
            src_ref=z_send.at[dz], dst_ref=z_recv.at[dz],
            send_sem=z_sem.at[0], recv_sem=z_sem.at[1],
            device_id=dev_z(dz), device_id_type=MESH,
        ).start()

    got = z_block(0)
    pltpu.make_async_copy(y_recv.at[pl.ds(1, NR - 1)], y_recv.at[pl.ds(1, NR - 1)], y_sem.at[0]).wait()
    pltpu.make_async_copy(idx_recv.at[pl.ds(1, NR - 1)], idx_recv.at[pl.ds(1, NR - 1)], idx_sem.at[0]).wait()
    for dx in (1, 2, 3):
        copy_x(dx).wait_send()

    z_in = z_recv.at[pl.ds(1, NZ - 1)]
    pltpu.make_async_copy(z_in, z_in, z_sem.at[1]).wait()
    for dz in range(1, NZ):
        got = got + z_recv[dz].astype(F32)
    hi = got.astype(BF16).astype(F32)
    right = jnp.concatenate([hi, got - hi, hi, jnp.zeros((104, 128), F32)], axis=0).astype(BF16)
    result = jnp.dot(left[...], right, preferred_element_type=F32)
    out_ref[...] = result.astype(BF16).reshape(2, 512, 128)
    pltpu.make_async_copy(z_in, z_in, z_sem.at[0]).wait()


def shards(
    occupied_index,
    doubles_slab,
    lambda_slab,
    aux_factors,
    dressed_factors,
    virtual_coefs,
    occupied_coefs,
):
    dma = pltpu.SemaphoreType.DMA
    return pl.pallas_call(
        kernel,
        out_shape=jax.ShapeDtypeStruct((2, 512, 128), BF16),
        in_specs=[pl.BlockSpec(memory_space=pltpu.HBM)] * 7,
        out_specs=pl.BlockSpec(memory_space=pltpu.VMEM),
        scratch_shapes=[
            pltpu.SMEM((1,), jnp.int32),
            pltpu.VMEM((256, 2048), BF16),
            pltpu.VMEM((256, 2048), BF16),
            pltpu.VMEM((256, 2048), BF16),
            pltpu.VMEM((256, 2048), BF16),
            pltpu.VMEM((1024, 256), BF16),
            pltpu.VMEM((4, 512), F32),
            pltpu.VMEM((2, 256, 128), F32),
            pltpu.VMEM((1, 128), jnp.int32),
            pltpu.VMEM((NR, 1, 128), jnp.int32),
            pltpu.VMEM((NR, 16, 256), BF16),
            pltpu.VMEM((NR, 16, 256), BF16),
            pltpu.VMEM((64, 256), BF16),
            pltpu.VMEM((8, 128), F32),
            pltpu.VMEM((NX - 1, 64, 256), BF16),
            pltpu.VMEM((NX - 1, 64, 256), BF16),
            pltpu.VMEM((8, 8, 256), F32),
            pltpu.VMEM((NZ, 8, 128), BF16),
            pltpu.VMEM((NZ, 8, 128), BF16),
            pltpu.VMEM((128, 1024), F32),
            pltpu.VMEM((1024, 128), BF16),
            dma((11,)),
            dma((2,)),
            dma((2,)),
            dma((2, NX - 1)),
            dma((2,)),
            pltpu.SemaphoreType.REGULAR,
        ],
        compiler_params=pltpu.CompilerParams(
            collective_id=0, has_side_effects=True, vmem_limit_bytes=32 << 20
        ),
    )(
        occupied_index, doubles_slab, lambda_slab, aux_factors, dressed_factors,
        virtual_coefs, occupied_coefs.T,
    )


def solution(mesh):
    placed = (
        P("pair"),
        P("pair", "aux", None),
        P("pair", "aux", None),
        P("pair", None, None),
        P("pair", None, None),
        P(None, "aux"),
        P(),
    )
    return jax.shard_map(
        shards, mesh=mesh, in_specs=placed, out_specs=P("pair", None, "aux"), check_vma=False
    )
```

time: 84.8 us -> 47.1 us (0.56)
  the two profiles are of different devices: /device:TPU:1 before, /device:TPU:8 now
where the time goes in v1:
time: 47.1 us; the launch traced here: 46.8 us
  Pallas kernels  38.8 us (82%)
  local copies, waits for them, and re-layouts  7.33 us (16%)
  between operations  0.67 us (1%)
    pallas_call x1, Pallas kernels, shards(): pl.pallas_call(kernel, out_shape=jax.ShapeDtypeStruct((2, 512, 128), BF16...  38.8 us
    unnamed x13, local copies, waits for them, and re-layouts  7.33 us

profile of v1, /device:TPU:8, one launch (start us, length us, event | category | flops | bytes accessed | tf_op | source)
XLA Modules:
  0.0 46.8 jit_solution(2547038999160991186)
XLA Ops:
  0.7 0.0 copy-start
  0.7 1.2 %copy-done = bf16[1,256,2048]{2,1,0:T(8,128)(2,1)S(1)} copy-done((bf16[1,256,2048]{2,1,0:T(8,128)(2,1)S(1)}, bf16[1,256,2048]{2,1,0:T(8,128)(2,1)}, u32[]{:S(2)}) %copy-start) | copy-done | bytes 1048600
  1.9 0.0 copy-start.1
  1.9 1.2 %copy-done.1 = bf16[1,256,2048]{2,1,0:T(8,128)(2,1)S(1)} copy-done((bf16[1,256,2048]{2,1,0:T(8,128)(2,1)S(1)}, bf16[1,256,2048]{2,1,0:T(8,128)(2,1)}, u32[]{:S(2)}) %copy-start.1) | copy-done | bytes 1048600
  3.1 0.0 copy-start.2
  3.1 1.2 %copy-done.2 = bf16[1,256,2048]{2,1,0:T(8,128)(2,1)S(1)} copy-done((bf16[1,256,2048]{2,1,0:T(8,128)(2,1)S(1)}, bf16[1,256,2048]{2,1,0:T(8,128)(2,1)}, u32[]{:S(2)}) %copy-start.2) | copy-done | bytes 1048600
  4.3 0.0 copy-start.3
  4.3 1.2 %copy-done.3 = bf16[1,256,2048]{2,1,0:T(8,128)(2,1)S(1)} copy-done((bf16[1,256,2048]{2,1,0:T(8,128)(2,1)S(1)}, bf16[1,256,2048]{2,1,0:T(8,128)(2,1)}, u32[]{:S(2)}) %copy-start.3) | copy-done | bytes 1048600
  5.6 0.0 copy-start.4
  5.6 1.0 %copy-done.4 = bf16[1024,256]{1,0:T(8,128)(2,1)S(1)} copy-done((bf16[1024,256]{1,0:T(8,128)(2,1)S(1)}, bf16[1024,256]{1,0:T(8,128)(2,1)}, u32[]{:S(2)}) %copy-start.4) | copy-done | bytes 524312
  6.6 0.0 copy-start.5
  6.6 0.7 %copy-done.5 = f32[512,4]{0,1:T(4,128)S(1)} copy-done((f32[512,4]{0,1:T(4,128)S(1)}, f32[512,4]{0,1:T(4,128)}, u32[]{:S(2)}) %copy-start.5) | copy-done | bytes 8216
  7.3 38.8 %shard_map.73 = bf16[2,512,128]{2,1,0:T(8,128)(2,1)S(1)} custom-call(s32[1]{0:T(128)S(6)} %copy.9.idx_hbm, bf16[1,256,2048]{2,1,0:T(8,128)(2,1)S(1)} %copy-done, bf16[1,256,2048]{2,1,0:T(8,128)(2,1)S(1)} %copy-done.1, bf16[1,256,2048]{2,1,0:T(8,128)(2,1)S(1)} %copy-done.2, bf16[1,256,2048]{2,1,0:T(8,128)(2,1)S(1)} %copy-done.3, ...), custom_call_target="tpu_custom_call" | custom-call | tf_op jit(solution)/shard_map/pallas_call | solution.py:239
  46.1 0.7 %copy.10 = bf16[2,512,128]{2,1,0:T(8,128)(2,1)} copy(bf16[2,512,128]{2,1,0:T(8,128)(2,1)S(1)} %shard_map.73) | data formatting | bytes 524288
Async XLA Ops:
  0.7 1.2 %copy-start = (bf16[1,256,2048]{2,1,0:T(8,128)(2,1)S(1)}, bf16[1,256,2048]{2,1,0:T(8,128)(2,1)}, u32[]{:S(2)}) copy-start(bf16[1,256,2048]{2,1,0:T(8,128)(2,1)} %d_hbm.1) | copy-start | bytes 3145732
  1.9 1.2 %copy-start.1 = (bf16[1,256,2048]{2,1,0:T(8,128)(2,1)S(1)}, bf16[1,256,2048]{2,1,0:T(8,128)(2,1)}, u32[]{:S(2)}) copy-start(bf16[1,256,2048]{2,1,0:T(8,128)(2,1)} %l_hbm.1) | copy-start | bytes 3145732
  3.1 1.2 %copy-start.2 = (bf16[1,256,2048]{2,1,0:T(8,128)(2,1)S(1)}, bf16[1,256,2048]{2,1,0:T(8,128)(2,1)}, u32[]{:S(2)}) copy-start(bf16[1,256,2048]{2,1,0:T(8,128)(2,1)} %f_hbm.1) | copy-start | bytes 3145732
  4.3 1.2 %copy-start.3 = (bf16[1,256,2048]{2,1,0:T(8,128)(2,1)S(1)}, bf16[1,256,2048]{2,1,0:T(8,128)(2,1)}, u32[]{:S(2)}) copy-start(bf16[1,256,2048]{2,1,0:T(8,128)(2,1)} %g_hbm.1) | copy-start | bytes 3145732
  5.6 1.0 %copy-start.4 = (bf16[1024,256]{1,0:T(8,128)(2,1)S(1)}, bf16[1024,256]{1,0:T(8,128)(2,1)}, u32[]{:S(2)}) copy-start(bf16[1024,256]{1,0:T(8,128)(2,1)} %v_hbm.1) | copy-start | bytes 1572868
  6.6 0.7 %copy-start.5 = (f32[512,4]{0,1:T(4,128)S(1)}, f32[512,4]{0,1:T(4,128)}, u32[]{:S(2)}) copy-start(f32[512,4]{0,1:T(4,128)} %param.13) | copy-start | bytes 24580

commit v2 on v1

v2 whole, which is shorter than its diff:
```python
import jax
import jax.numpy as jnp
from jax import lax
from jax.experimental import pallas as pl
from jax.experimental.pallas import tpu as pltpu
from jax.sharding import PartitionSpec as P

MESH = pl.DeviceIdType.MESH
F32, BF16 = jnp.float32, jnp.bfloat16
NT = (((1,), (1,)), ((), ()))
NX, NY, NZ, ZL = 4, 8, 16, 8
NR = 2 * NY
VMEM_KIB = 60 << 10


def device(x, y, z, core):
    pair = (lax.rem(z, ZL) * NY + y) * 2 + core
    aux = x * 2 + lax.div(z, ZL)
    return (pair, aux)


def kernel(
    idx_hbm, d_hbm, l_hbm, f_hbm, g_hbm, v_hbm, c_hbm, out_ref,
    idx_s, d_v, l_v, f_v, g_v, v_v, c_v,
    prod, idx_send, idx_recv, y_send, y_recv, sel, x_send, x_recv,
    total, z_send, z_recv, wide, left,
    load_sem, idx_sem, y_sem, x_sem, z_sem, ready_sem,
):
    pair, aux = lax.axis_index("pair"), lax.axis_index("aux")
    core = lax.rem(pair, 2)
    y = lax.rem(lax.div(pair, 2), NY)
    x = lax.div(aux, 2)
    z = lax.rem(aux, 2) * ZL + lax.div(pair, NR)
    barrier = pltpu.get_barrier_semaphore()

    def rel_y(dy, dc):
        return lax.rem(y + dy, NY), lax.rem(core + dc, 2)

    def dev_y(dy, dc):
        to_y, to_core = rel_y(dy, dc)
        return device(x, to_y, z, to_core)

    def dev_x(dx):
        return device(lax.rem(x + dx, NX), y, z, core)

    def dev_z(dz):
        return device(x, y, lax.rem(z + dz, NZ), core)

    def greet(to):
        pl.semaphore_signal(barrier, inc=1, device_id=to, device_id_type=MESH)

    @pl.loop(1, NR)
    def _(s):
        greet(dev_y(lax.div(s, 2), lax.rem(s, 2)))

    @pl.loop(1, NX)
    def _(s):
        greet(dev_x(s))

    @pl.loop(1, 5)
    def _(s):
        greet(dev_z(s))
        greet(dev_z(NZ - s))

    def load(src, dst, n):
        return pltpu.make_async_copy(src, dst, load_sem.at[n])

    load_i = load(idx_hbm, idx_s, 0)
    load_i.start()
    depth = d_v.shape[1] // 2
    loads = []
    for a_hbm, a_v, b_hbm, b_v in ((f_hbm, f_v, d_hbm, d_v), (g_hbm, g_v, l_hbm, l_v)):
        for k in range(2):
            cols = pl.ds(k * depth, depth)
            top = pl.ds(0, 128)
            n = 1 + 2 * len(loads)
            loads.append((
                load(b_hbm.at[0, :, cols], b_v.at[:, cols], n),
                load(a_hbm.at[0, top, cols], a_v.at[top, cols], n + 1),
            ))
    rest = pl.ds(128, 128)
    later = [
        load(f_hbm.at[0, rest, :], f_v.at[rest, :], 9),
        load(g_hbm.at[0, rest, :], g_v.at[rest, :], 10),
    ]
    load_v = load(v_hbm, v_v, 11)
    load_c = load(c_hbm, c_v, 12)
    for pair_of in loads:
        for one in pair_of:
            one.start()
    for one in later:
        one.start()
    load_v.start()
    load_c.start()

    def pack(t, acc):
        prod[0] = acc[:, :128]
        prod[1] = acc[:, 128:]
        for r in range(NR):
            for j in range(2):
                even = prod[j, pl.ds(2 * r, 4, stride=32), :]
                odd = prod[j, pl.ds(2 * r + 1, 4, stride=32), :]
                both = jnp.concatenate([even, odd], axis=0).astype(BF16)
                y_send[t, r, :, j * 128 : (j + 1) * 128] = both
        y_recv[t, 0] = y_send[t, y * 2 + core]

    def send_y(t, to_y, to_core):
        dy, dc = lax.rem(to_y - y + NY, NY), lax.rem(to_core + core, 2)
        slot = dy * 2 + dc

        @pl.when(slot != 0)
        def _():
            to = device(x, to_y, z, to_core)
            if t == 0:
                pltpu.make_async_remote_copy(
                    src_ref=idx_send, dst_ref=idx_recv.at[slot],
                    send_sem=idx_sem.at[0], recv_sem=idx_sem.at[1],
                    device_id=to, device_id_type=MESH,
                ).start()
            pltpu.make_async_remote_copy(
                src_ref=y_send.at[t, to_y * 2 + to_core], dst_ref=y_recv.at[t, slot],
                send_sem=y_sem.at[0, t], recv_sem=y_sem.at[1, t],
                device_id=to, device_id_type=MESH,
            ).start()

    def send_all_y(t):
        @pl.loop(0, NY // 2)
        def _(k):
            send_y(t, k, 0)
            send_y(t, k, 1)

        @pl.loop(0, NY // 2)
        def _(k):
            send_y(t, NY - 1 - k, 0)
            send_y(t, NY - 1 - k, 1)

    acc = None
    for n, (load_b, load_a) in enumerate(loads):
        load_b.wait()
        load_a.wait()
        a_v, b_v = ((f_v, d_v), (g_v, l_v))[n // 2]
        cols = slice(n % 2 * depth, (n % 2 + 1) * depth)
        part = lax.dot_general(a_v[:128, cols], b_v[:, cols], NT, preferred_element_type=F32)
        acc = part if acc is None else acc + part
    pack(0, acc)
    load_i.wait()
    idx_send[...] = jnp.full((1, 128), idx_s[0, 0], jnp.int32)
    idx_recv[0] = jnp.full((1, 128), idx_s[0, 0], jnp.int32)

    pl.semaphore_wait(barrier, NR - 1 + NX - 1 + 8)
    send_all_y(0)
    for dz in (4, NZ - 4):
        pl.semaphore_signal(ready_sem, inc=1, device_id=dev_z(dz), device_id_type=MESH)

    later[0].wait()
    acc = lax.dot_general(f_v[128:, :], d_v[...], NT, preferred_element_type=F32)
    later[1].wait()
    acc = acc + lax.dot_general(g_v[128:, :], l_v[...], NT, preferred_element_type=F32)
    pack(1, acc)
    send_all_y(1)

    load_c.wait()
    wide[...] = jnp.zeros_like(wide)
    c_hi = c_v[...].astype(BF16).astype(F32)
    c_lo = (c_v[...] - c_hi)
    for e in range(2):
        cols = slice(e * 512, (e + 1) * 512)
        for i in range(4):
            row = i * 2 + e
            wide[row : row + 1, cols] = c_hi[i : i + 1, :]
            wide[8 + row : 9 + row, cols] = c_hi[i : i + 1, :]
            wide[16 + row : 17 + row, cols] = c_lo[i : i + 1, :]
    left[...] = wide[...].T.astype(BF16)

    others = idx_recv.at[pl.ds(1, NR - 1)]
    pltpu.make_async_copy(others, others, idx_sem.at[1]).wait()
    row = lax.broadcasted_iota(jnp.int32, (32, 128), 0)
    col = lax.broadcasted_iota(jnp.int32, (32, 128), 1)
    same = ((row >> 3) == (col & 3)) & ((row & 1) == ((col >> 2) & 1))
    lane = lax.broadcasted_iota(jnp.int32, (1, 128), 1) >> 3
    which = jnp.zeros((1, 128), jnp.int32)
    for s in range(NR):
        which = which + idx_recv[s] * (lane == s).astype(jnp.int32)
    match = same.astype(F32) * (which == ((row >> 1) & 3)).astype(F32)
    sel[...] = match.astype(BF16)
    load_v.wait()

    def copy_x(t, hi, dx):
        return pltpu.make_async_remote_copy(
            src_ref=x_send.at[t, hi, dx - 1], dst_ref=x_recv.at[t, hi, dx - 1],
            send_sem=x_sem.at[0, t, hi, dx - 1], recv_sem=x_sem.at[1, t, hi, dx - 1],
            device_id=dev_x(dx), device_id_type=MESH,
        )

    own = {}

    def turn(t):
        others = y_recv.at[t, pl.ds(1, NR - 1)]
        pltpu.make_async_copy(others, others, y_sem.at[1, t]).wait()
        arrived = y_recv[t].reshape(128, 256)
        summed = jnp.dot(sel[...], arrived, preferred_element_type=F32).astype(BF16)

        def turned(hi, dx):
            first = lax.rem(x + dx, NX) * 256 + hi * 128
            rows = pl.ds(pl.multiple_of(first, 128), 128)
            return lax.dot_general(summed, v_v[rows, :], NT, preferred_element_type=F32)

        for hi in range(2):
            for dx in (2, 1, 3):
                x_send[t, hi, dx - 1] = turned(hi, dx).astype(BF16)
            for dx in (2, 1, 3):
                copy_x(t, hi, dx).start()
        for hi in range(2):
            own[t, hi] = turned(hi, 0)

    def pass_on(t, hi):
        mine = own[t, hi]
        for dx in (1, 3, 2):
            copy_x(t, hi, dx).wait_recv()
            mine = mine + x_recv[t, hi, dx - 1].astype(F32)
        blocks = mine.reshape(4, 8, 128)
        total[hi, t * 4 : t * 4 + 4] = blocks
        z_send[hi, t * 4 : t * 4 + 4] = blocks.astype(BF16)

    def send_z(t, hi):
        @pl.loop(t * 4, t * 4 + 4)
        def _(to_l):
            to_z = hi * ZL + to_l
            dz = lax.rem(to_z - z + NZ, NZ)

            @pl.when(dz != 0)
            def _():
                pltpu.make_async_remote_copy(
                    src_ref=z_send.at[hi, to_l], dst_ref=z_recv.at[dz],
                    send_sem=z_sem.at[0], recv_sem=z_sem.at[1],
                    device_id=dev_z(dz), device_id_type=MESH,
                ).start()

    turn(0)
    pass_on(0, 0)
    pl.semaphore_wait(ready_sem, 2)
    send_z(0, 0)
    turn(1)
    for t, hi in ((0, 1), (1, 0), (1, 1)):
        pass_on(t, hi)
        send_z(t, hi)

    got = total[lax.div(z, ZL), lax.rem(z, ZL)]
    pltpu.make_async_copy(others, others, idx_sem.at[0]).wait()
    for t in range(2):
        sent = y_recv.at[t, pl.ds(1, NR - 1)]
        pltpu.make_async_copy(sent, sent, y_sem.at[0, t]).wait()
        for hi in range(2):
            for dx in (1, 2, 3):
                copy_x(t, hi, dx).wait_send()

    z_in = z_recv.at[pl.ds(1, NZ - 1)]
    pltpu.make_async_copy(z_in, z_in, z_sem.at[1]).wait()
    for dz in range(1, NZ):
        got = got + z_recv[dz].astype(F32)
    hi = got.astype(BF16).astype(F32)
    right = jnp.concatenate([hi, got - hi, hi, jnp.zeros((104, 128), F32)], axis=0).astype(BF16)
    result = jnp.dot(left[...], right, preferred_element_type=F32)
    out_ref[...] = result.astype(BF16).reshape(2, 512, 128)
    pltpu.make_async_copy(z_in, z_in, z_sem.at[0]).wait()


def shards(
    occupied_index,
    doubles_slab,
    lambda_slab,
    aux_factors,
    dressed_factors,
    virtual_coefs,
    occupied_coefs,
):
    dma = pltpu.SemaphoreType.DMA
    return pl.pallas_call(
        kernel,
        out_shape=pltpu.VMEM((2, 512, 128), BF16),
        in_specs=[pl.BlockSpec(memory_space=pltpu.HBM)] * 7,
        out_specs=pl.BlockSpec(memory_space=pltpu.VMEM),
        scratch_shapes=[
            pltpu.SMEM((1, 1), jnp.int32),
            pltpu.VMEM((256, 2048), BF16),
            pltpu.VMEM((256, 2048), BF16),
            pltpu.VMEM((256, 2048), BF16),
            pltpu.VMEM((256, 2048), BF16),
            pltpu.VMEM((1024, 256), BF16),
            pltpu.VMEM((4, 512), F32),
            pltpu.VMEM((2, 128, 128), F32),
            pltpu.VMEM((1, 128), jnp.int32),
            pltpu.VMEM((NR, 1, 128), jnp.int32),
            pltpu.VMEM((2, NR, 8, 256), BF16),
            pltpu.VMEM((2, NR, 8, 256), BF16),
            pltpu.VMEM((32, 128), BF16),
            pltpu.VMEM((2, 2, NX - 1, 32, 128), BF16),
            pltpu.VMEM((2, 2, NX - 1, 32, 128), BF16),
            pltpu.VMEM((2, 8, 8, 128), F32),
            pltpu.VMEM((2, 8, 8, 128), BF16),
            pltpu.VMEM((NZ, 8, 128), BF16),
            pltpu.VMEM((128, 1024), F32),
            pltpu.VMEM((1024, 128), BF16),
            dma((13,)),
            dma((2,)),
            dma((2, 2)),
            dma((2, 2, 2, NX - 1)),
            dma((2,)),
            pltpu.SemaphoreType.REGULAR,
        ],
        compiler_params=pltpu.CompilerParams(
            collective_id=0, has_side_effects=True, vmem_limit_bytes=VMEM_KIB << 10
        ),
    )(
        occupied_index.reshape(1, 1), doubles_slab, lambda_slab, aux_factors, dressed_factors,
        virtual_coefs, occupied_coefs.T,
    )


def solution(mesh):
    placed = (
        P("pair"),
        P("pair", "aux", None),
        P("pair", "aux", None),
        P("pair", None, None),
        P("pair", None, None),
        P(None, "aux"),
        P(),
    )
    return jax.shard_map(
        shards, mesh=mesh, in_specs=placed, out_specs=P("pair", None, "aux"), check_vma=False
    )
```

time: 47.1 us -> 38.9 us (0.83)
  the two profiles are of different devices: /device:TPU:8 before, /device:TPU:1 now
where the time goes in v2:
time: 38.9 us; the launch traced here: 38.8 us
  Pallas kernels  37.4 us (96%)
  local copies, waits for them, and re-layouts  0.71 us (2%)
  between operations  0.66 us (2%)
    pallas_call x1, Pallas kernels, shards(): pl.pallas_call(kernel, out_shape=pltpu.VMEM((2, 512, 128), BF16), in_spec...  37.4 us

profile of v2, /device:TPU:1, one launch (start us, length us, event | category | flops | bytes accessed | tf_op | source)
XLA Modules:
  0.0 38.8 jit_solution(2065156792928311253)
XLA Ops:
  0.7 37.4 %shard_map.73 = bf16[2,512,128]{2,1,0:T(8,128)(2,1)S(1)} custom-call(s32[1,1]{1,0:T(1,128)} %bitcast.2.idx_hbm, bf16[1,256,2048]{2,1,0:T(8,128)(2,1)} %d_hbm.1, bf16[1,256,2048]{2,1,0:T(8,128)(2,1)} %l_hbm.1, bf16[1,256,2048]{2,1,0:T(8,128)(2,1)} %f_hbm.1, bf16[1,256,2048]{2,1,0:T(8,128)(2,1)} %g_hbm.1, bf16[1024,256]{1,0:T(8,128)(2,1)} %v_hbm.1, ...), custom_call_target="tpu_custom_call" | custom-call | tf_op jit(solution)/shard_map/pallas_call | solution.py:278
  38.1 0.7 %copy.9 = bf16[2,512,128]{2,1,0:T(8,128)(2,1)} copy(bf16[2,512,128]{2,1,0:T(8,128)(2,1)S(1)} %shard_map.73) | data formatting | bytes 524288

commit v3 on v2

v3 whole, which is shorter than its diff:
```python
import jax
import jax.numpy as jnp
from jax import lax
from jax.experimental import pallas as pl
from jax.experimental.pallas import tpu as pltpu
from jax.sharding import PartitionSpec as P

MESH = pl.DeviceIdType.MESH
F32, BF16 = jnp.float32, jnp.bfloat16
NT = (((1,), (1,)), ((), ()))
NX, NY, NZ, ZL = 4, 8, 16, 8
NR = 2 * NY
Y_ORDER = (0, 1, 2, 3, 7, 6, 5, 4)
X_ORDER = (0, 1, 2, 3)


def kernel(
    idx_hbm, d_hbm, l_hbm, f_hbm, g_hbm, v_hbm, c_hbm, out_ref,
    idx_s, d_v, l_v, f_v, g_v, v_v, c_v,
    order, idx_send, idx_recv, y_send, y_recv, sel, x_send, x_recv,
    z_send, z_recv, wide, left,
    load_sem, idx_sem, y_sem, x_sem, z_sem, ready_sem,
):
    pair, aux = lax.axis_index("pair"), lax.axis_index("aux")
    barrier = pltpu.get_barrier_semaphore()

    def load(src, dst, n):
        return pltpu.make_async_copy(src, dst, load_sem.at[n])

    depth = d_v.shape[1] // 2
    loads = []
    for a_hbm, a_v, b_hbm, b_v in ((f_hbm, f_v, d_hbm, d_v), (g_hbm, g_v, l_hbm, l_v)):
        for k in range(2):
            cols = pl.ds(k * depth, depth)
            top = pl.ds(0, 128)
            n = 1 + 2 * len(loads)
            loads.append((
                load(b_hbm.at[0, :, cols], b_v.at[:, cols], n),
                load(a_hbm.at[0, top, cols], a_v.at[top, cols], n + 1),
            ))
    rest = pl.ds(128, 128)
    later = [
        load(f_hbm.at[0, rest, :], f_v.at[rest, :], 9),
        load(g_hbm.at[0, rest, :], g_v.at[rest, :], 10),
    ]
    load_i = load(idx_hbm, idx_s, 0)
    load_v = [load(v_hbm.at[:, hi], v_v.at[hi], 11 + hi) for hi in range(2)]
    load_c = load(c_hbm, c_v, 13)
    for pair_of in loads:
        for one in pair_of:
            one.start()
    load_i.start()

    r = lax.rem(pair, NR)
    l = lax.div(pair, NR)
    x = lax.div(aux, 2)
    h = lax.rem(aux, 2)
    z = h * ZL + l
    row0 = l * NR

    def z_away(dz):
        to_z = lax.rem(z + (dz + NZ), NZ)
        to_h = lax.div(to_z, ZL)
        return ((to_z - to_h * ZL) * NR + r, x * 2 + to_h)

    def greet(to):
        pl.semaphore_signal(barrier, inc=1, device_id=to, device_id_type=MESH)

    for to_r in range(NR):
        @pl.when(r != to_r)
        def _():
            greet((row0 + to_r, aux))

    for to_x in range(NX):
        @pl.when(x != to_x)
        def _():
            greet((pair, to_x * 2 + h))

    for dz in range(1, 3):
        greet(z_away(dz))
        greet(z_away(-dz))

    for one in later + load_v + [load_c]:
        one.start()

    row = lax.broadcasted_iota(jnp.int32, (128, 128), 0)
    col = lax.broadcasted_iota(jnp.int32, (128, 128), 1)
    source = (row & 3) * 32 + (row >> 3) * 2 + ((row >> 2) & 1)
    order[...] = (source == col).astype(F32).astype(BF16)

    def pack(t, acc):
        sorted_rows = jnp.dot(order[...], acc.astype(BF16), preferred_element_type=F32)
        y_send[t] = sorted_rows.astype(BF16).reshape(NR, 8, 256)
        y_recv[t, r] = y_send[t, r]

    def send_y(t):
        for to_r in (2 * to_y + c for to_y in Y_ORDER for c in range(2)):
            @pl.when(r != to_r)
            def _():
                to = (row0 + to_r, aux)
                if t == 0:
                    pltpu.make_async_remote_copy(
                        src_ref=idx_send, dst_ref=idx_recv.at[r],
                        send_sem=idx_sem.at[0], recv_sem=idx_sem.at[1],
                        device_id=to, device_id_type=MESH,
                    ).start()
                pltpu.make_async_remote_copy(
                    src_ref=y_send.at[t, to_r], dst_ref=y_recv.at[t, r],
                    send_sem=y_sem.at[0, t], recv_sem=y_sem.at[1, t],
                    device_id=to, device_id_type=MESH,
                ).start()

    def relay(n, dz):
        for to in (z_away(dz), z_away(-dz)):
            pl.semaphore_signal(ready_sem.at[n], inc=1, device_id=to, device_id_type=MESH)

    def settle(ref, sem):
        pltpu.make_async_copy(ref, ref, sem).wait()

    acc = None
    for n, (load_b, load_a) in enumerate(loads):
        load_b.wait()
        load_a.wait()
        a_v, b_v = ((f_v, d_v), (g_v, l_v))[n // 2]
        cols = slice(n % 2 * depth, (n % 2 + 1) * depth)
        part = lax.dot_general(a_v[:128, cols], b_v[:, cols], NT, preferred_element_type=F32)
        acc = part if acc is None else acc + part
    pack(0, acc)
    load_i.wait()
    idx_send[...] = jnp.full((1, 128), idx_s[0, 0], jnp.int32)
    idx_recv[r] = jnp.full((1, 128), idx_s[0, 0], jnp.int32)

    pl.semaphore_wait(barrier, NR - 1 + NX - 1 + 4)
    send_y(0)
    relay(0, 2)

    later[0].wait()
    acc = lax.dot_general(f_v[128:, :], d_v[...], NT, preferred_element_type=F32)
    later[1].wait()
    acc = acc + lax.dot_general(g_v[128:, :], l_v[...], NT, preferred_element_type=F32)
    pack(1, acc)
    send_y(1)

    load_c.wait()
    wide[...] = jnp.zeros_like(wide)
    c_hi = c_v[...].astype(BF16).astype(F32)
    c_lo = c_v[...] - c_hi
    for e in range(2):
        cols = slice(e * 512, (e + 1) * 512)
        for i in range(4):
            row = i * 2 + e
            wide[row : row + 1, cols] = c_hi[i : i + 1, :]
            wide[8 + row : 9 + row, cols] = c_hi[i : i + 1, :]
            wide[16 + row : 17 + row, cols] = c_lo[i : i + 1, :]
    left[...] = wide[...].T.astype(BF16)

    settle(idx_recv.at[pl.ds(0, NR - 1)], idx_sem.at[1])
    row = lax.broadcasted_iota(jnp.int32, (32, 128), 0)
    col = lax.broadcasted_iota(jnp.int32, (32, 128), 1)
    same = ((row >> 3) == (col & 3)) & ((row & 1) == ((col >> 2) & 1))
    lane = lax.broadcasted_iota(jnp.int32, (1, 128), 1) >> 3
    which = jnp.zeros((1, 128), jnp.int32)
    for s in range(NR):
        which = which + idx_recv[s] * (lane == s).astype(jnp.int32)
    match = same.astype(F32) * (which == ((row >> 1) & 3)).astype(F32)
    sel[...] = match.astype(BF16)
    for one in load_v:
        one.wait()

    def turn(t):
        settle(y_recv.at[t, pl.ds(0, NR - 1)], y_sem.at[1, t])
        arrived = y_recv[t].reshape(128, 256)
        summed = jnp.dot(sel[...], arrived, preferred_element_type=F32).astype(BF16)
        for hi in range(2):
            for to_x in X_ORDER:
                turned = lax.dot_general(summed, v_v[hi, to_x], NT, preferred_element_type=F32)
                x_send[t, hi, to_x] = turned.astype(BF16)
            for to_x in X_ORDER:
                @pl.when(x != to_x)
                def _():
                    pltpu.make_async_remote_copy(
                        src_ref=x_send.at[t, hi, to_x], dst_ref=x_recv.at[t, hi, x],
                        send_sem=x_sem.at[0, t, hi], recv_sem=x_sem.at[1, t, hi],
                        device_id=(pair, to_x * 2 + h), device_id_type=MESH,
                    ).start()
            x_recv[t, hi, x] = x_send[t, hi, x]

    def pass_on(t, hi):
        settle(x_recv.at[t, hi, pl.ds(0, NX - 1)], x_sem.at[1, t, hi])
        total = x_recv[t, hi, 0].astype(F32)
        for from_x in range(1, NX):
            total = total + x_recv[t, hi, from_x].astype(F32)
        z_send[hi, t * 4 : t * 4 + 4] = total.reshape(4, 8, 128).astype(BF16)

    def send_z(t, hi):
        for to_l in range(t * 4, t * 4 + 4):
            @pl.when(z != hi * ZL + to_l)
            def _():
                pltpu.make_async_remote_copy(
                    src_ref=z_send.at[hi, to_l], dst_ref=z_recv.at[z],
                    send_sem=z_sem.at[0], recv_sem=z_sem.at[1],
                    device_id=(to_l * NR + r, x * 2 + hi), device_id_type=MESH,
                ).start()

    pl.semaphore_wait(ready_sem.at[0], 2)
    relay(1, 4)
    turn(0)
    turn(1)
    pass_on(0, 0)
    pl.semaphore_wait(ready_sem.at[1], 2)
    send_z(0, 0)
    for t, hi in ((1, 0), (0, 1), (1, 1)):
        pass_on(t, hi)
        send_z(t, hi)
    z_recv[z] = z_send[h, l]

    settle(idx_recv.at[pl.ds(0, NR - 1)], idx_sem.at[0])
    for t in range(2):
        settle(y_recv.at[t, pl.ds(0, NR - 1)], y_sem.at[0, t])
        for hi in range(2):
            settle(x_recv.at[t, hi, pl.ds(0, NX - 1)], x_sem.at[0, t, hi])

    settle(z_recv.at[pl.ds(0, NZ - 1)], z_sem.at[1])
    got = z_recv[0].astype(F32)
    for from_z in range(1, NZ):
        got = got + z_recv[from_z].astype(F32)
    hi = got.astype(BF16).astype(F32)
    right = jnp.concatenate([hi, got - hi, hi, jnp.zeros((104, 128), F32)], axis=0).astype(BF16)
    result = jnp.dot(left[...], right, preferred_element_type=F32)
    out_ref[...] = result.astype(BF16).reshape(2, 512, 128)
    settle(z_recv.at[pl.ds(0, NZ - 1)], z_sem.at[0])


def shards(
    occupied_index,
    doubles_slab,
    lambda_slab,
    aux_factors,
    dressed_factors,
    virtual_coefs,
    occupied_coefs,
):
    dma = pltpu.SemaphoreType.DMA
    return pl.pallas_call(
        kernel,
        out_shape=pltpu.VMEM((2, 512, 128), BF16),
        in_specs=[pl.BlockSpec(memory_space=pltpu.HBM)] * 7,
        out_specs=pl.BlockSpec(memory_space=pltpu.VMEM),
        scratch_shapes=[
            pltpu.SMEM((1, 1), jnp.int32),
            pltpu.VMEM((256, 2048), BF16),
            pltpu.VMEM((256, 2048), BF16),
            pltpu.VMEM((256, 2048), BF16),
            pltpu.VMEM((256, 2048), BF16),
            pltpu.VMEM((2, NX, 128, 256), BF16),
            pltpu.VMEM((4, 512), F32),
            pltpu.VMEM((128, 128), BF16),
            pltpu.VMEM((1, 128), jnp.int32),
            pltpu.VMEM((NR, 1, 128), jnp.int32),
            pltpu.VMEM((2, NR, 8, 256), BF16),
            pltpu.VMEM((2, NR, 8, 256), BF16),
            pltpu.VMEM((32, 128), BF16),
            pltpu.VMEM((2, 2, NX, 32, 128), BF16),
            pltpu.VMEM((2, 2, NX, 32, 128), BF16),
            pltpu.VMEM((2, ZL, 8, 128), BF16),
            pltpu.VMEM((NZ, 8, 128), BF16),
            pltpu.VMEM((128, 1024), F32),
            pltpu.VMEM((1024, 128), BF16),
            dma((14,)),
            dma((2,)),
            dma((2, 2)),
            dma((2, 2, 2)),
            dma((2,)),
            pltpu.SemaphoreType.REGULAR((2,)),
        ],
        compiler_params=pltpu.CompilerParams(
            collective_id=0, has_side_effects=True, vmem_limit_bytes=60 << 20
        ),
    )(
        occupied_index.reshape(1, 1), doubles_slab, lambda_slab, aux_factors, dressed_factors,
        virtual_coefs.reshape(NX, 2, 128, 256), occupied_coefs.T,
    )


def solution(mesh):
    placed = (
        P("pair"),
        P("pair", "aux", None),
        P("pair", "aux", None),
        P("pair", None, None),
        P("pair", None, None),
        P(None, "aux"),
        P(),
    )
    return jax.shard_map(
        shards, mesh=mesh, in_specs=placed, out_specs=P("pair", None, "aux"), check_vma=False
    )
```

time: 38.9 us -> 37.1 us (0.954)
  Pallas kernels: 37.4 us -> 35.6 us
    pallas_call x1, Pallas kernels: 37.4 us -> 35.6 us  [shards(): pl.pallas_call(kernel, out_shape=pltpu.VMEM((2, 512, 128), BF16), in_spec...]
where the time goes in v3:
time: 37.1 us; the launch traced here: 36.9 us
  Pallas kernels  35.6 us (96%)
  local copies, waits for them, and re-layouts  0.71 us (2%)
  between operations  0.66 us (2%)
    pallas_call x1, Pallas kernels, shards(): pl.pallas_call(kernel, out_shape=pltpu.VMEM((2, 512, 128), BF16), in_spec...  35.6 us

profile of v3, /device:TPU:1, one launch (start us, length us, event | category | flops | bytes accessed | tf_op | source)
XLA Modules:
  0.0 36.9 jit_solution(14121434066959886357)
XLA Ops:
  0.7 35.6 %shard_map.73 = bf16[2,512,128]{2,1,0:T(8,128)(2,1)S(1)} custom-call(s32[1,1]{1,0:T(1,128)} %bitcast.3.idx_hbm, bf16[1,256,2048]{2,1,0:T(8,128)(2,1)} %d_hbm.1, bf16[1,256,2048]{2,1,0:T(8,128)(2,1)} %l_hbm.1, bf16[1,256,2048]{2,1,0:T(8,128)(2,1)} %f_hbm.1, bf16[1,256,2048]{2,1,0:T(8,128)(2,1)} %g_hbm.1, bf16[4,2,128,256]{3,2,1,0:T(8,128)(2,1)} %bitcast.4, ...), custom_call_target="tpu_custom_call" | custom-call | tf_op jit(solution)/shard_map/pallas_call | solution.py:244
  36.2 0.7 %copy.9 = bf16[2,512,128]{2,1,0:T(8,128)(2,1)} copy(bf16[2,512,128]{2,1,0:T(8,128)(2,1)S(1)} %shard_map.73) | data formatting | bytes 524288

commit v4 on v3

--- a/solution.py
+++ b/solution.py
@@ -76,12 +76,8 @@
         def _():
             greet((pair, to_x * 2 + h))
 
-    for dz in range(1, 3):
-        greet(z_away(dz))
-        greet(z_away(-dz))
-
-    for one in later + load_v + [load_c]:
-        one.start()
+    greet(z_away(1))
+    greet(z_away(-1))
 
     row = lax.broadcasted_iota(jnp.int32, (128, 128), 0)
     col = lax.broadcasted_iota(jnp.int32, (128, 128), 1)
@@ -121,6 +117,12 @@
     for n, (load_b, load_a) in enumerate(loads):
         load_b.wait()
         load_a.wait()
+        if n == 2:
+            for one in later:
+                one.start()
+        if n == 3:
+            for one in load_v + [load_c]:
+                one.start()
         a_v, b_v = ((f_v, d_v), (g_v, l_v))[n // 2]
         cols = slice(n % 2 * depth, (n % 2 + 1) * depth)
         part = lax.dot_general(a_v[:128, cols], b_v[:, cols], NT, preferred_element_type=F32)
@@ -130,9 +132,9 @@
     idx_send[...] = jnp.full((1, 128), idx_s[0, 0], jnp.int32)
     idx_recv[r] = jnp.full((1, 128), idx_s[0, 0], jnp.int32)
 
-    pl.semaphore_wait(barrier, NR - 1 + NX - 1 + 4)
+    pl.semaphore_wait(barrier, NR - 1 + NX - 1 + 2)
     send_y(0)
-    relay(0, 2)
+    relay(0, 1)
 
     later[0].wait()
     acc = lax.dot_general(f_v[128:, :], d_v[...], NT, preferred_element_type=F32)
@@ -140,6 +142,8 @@
     acc = acc + lax.dot_general(g_v[128:, :], l_v[...], NT, preferred_element_type=F32)
     pack(1, acc)
     send_y(1)
+    pl.semaphore_wait(ready_sem.at[0], 2)
+    relay(1, 2)
 
     load_c.wait()
     wide[...] = jnp.zeros_like(wide)
@@ -202,12 +206,12 @@
                     device_id=(to_l * NR + r, x * 2 + hi), device_id_type=MESH,
                 ).start()
 
-    pl.semaphore_wait(ready_sem.at[0], 2)
-    relay(1, 4)
+    pl.semaphore_wait(ready_sem.at[1], 2)
+    relay(2, 4)
     turn(0)
     turn(1)
     pass_on(0, 0)
-    pl.semaphore_wait(ready_sem.at[1], 2)
+    pl.semaphore_wait(ready_sem.at[2], 2)
     send_z(0, 0)
     for t, hi in ((1, 0), (0, 1), (1, 1)):
         pass_on(t, hi)
@@ -271,7 +275,7 @@
             dma((2, 2)),
             dma((2, 2, 2)),
             dma((2,)),
-            pltpu.SemaphoreType.REGULAR((2,)),
+            pltpu.SemaphoreType.REGULAR((3,)),
         ],
         compiler_params=pltpu.CompilerParams(
             collective_id=0, has_side_effects=True, vmem_limit_bytes=60 << 20

time: 37.1 us -> 37.1 us (level)
  no operation moved by 1% of the time
where the time goes in v4:
time: 37.1 us; the launch traced here: 36.9 us
  Pallas kernels  35.6 us (96%)
  local copies, waits for them, and re-layouts  0.71 us (2%)
  between operations  0.66 us (2%)
    pallas_call x1, Pallas kernels, shards(): pl.pallas_call(kernel, out_shape=pltpu.VMEM((2, 512, 128), BF16), in_spec...  35.6 us

profile of v4, /device:TPU:1, one launch (start us, length us, event | category | flops | bytes accessed | tf_op | source)
XLA Modules:
  0.0 36.9 jit_solution(12597648718524341064)
XLA Ops:
  0.7 35.6 %shard_map.73 = bf16[2,512,128]{2,1,0:T(8,128)(2,1)S(1)} custom-call(s32[1,1]{1,0:T(1,128)} %bitcast.3.idx_hbm, bf16[1,256,2048]{2,1,0:T(8,128)(2,1)} %d_hbm.1, bf16[1,256,2048]{2,1,0:T(8,128)(2,1)} %l_hbm.1, bf16[1,256,2048]{2,1,0:T(8,128)(2,1)} %f_hbm.1, bf16[1,256,2048]{2,1,0:T(8,128)(2,1)} %g_hbm.1, bf16[4,2,128,256]{3,2,1,0:T(8,128)(2,1)} %bitcast.4, ...), custom_call_target="tpu_custom_call" | custom-call | tf_op jit(solution)/shard_map/pallas_call | solution.py:248
  36.2 0.7 %copy.9 = bf16[2,512,128]{2,1,0:T(8,128)(2,1)} copy(bf16[2,512,128]{2,1,0:T(8,128)(2,1)S(1)} %shard_map.73) | data formatting | bytes 524288
